TPU v7x, 256 devices: a whole 4x4x8 slice. The times are simulated.
256 devices in a mesh: walker: 16 (over x, y), tangent: 8 (over z), feat: 2 (over core).
Axes of the slice: x: 4, y: 4, z: 8, core: 2. Of those that a mesh axis runs over, the one named last changes fastest.
Arguments:
- value_in: bfloat16 [512, 512], P('walker', 'feat'), may hold values from -0.94921875 to 0.94921875
- tang_in: bfloat16 [512, 768, 512], P('walker', 'tangent', 'feat'), may hold values from -1.01 to 1.01
- lap_in: bfloat16 [512, 512], P('walker', 'feat'), may hold values from -6 to 6
- w_first: bfloat16 [512, 512], P(('walker', 'tangent', 'feat')), may hold values from -0.25 to 0.25
- b_first: float32 [512], replicated, may hold values from -3 to 3
- w_second: bfloat16 [512, 512], P(('walker', 'tangent', 'feat')), may hold values from -0.25 to 0.25
- b_second: float32 [512], replicated, may hold values from -3 to 3
- readout: float32 [512], replicated, may hold values from -0.6 to 0.6
Outputs:
- log_amplitude: float32 [512], P('walker')
- gradient: float32 [512, 768], P('walker', 'tangent')
- kinetic: float32 [512], P('walker')
All inputs are finite; a program needn't handle non-finite values.
Results may differ from a plain program's by a relative error of at most 0.0044.
Values may be sent and summed in bfloat16 or wider, within the bound.
No kernel may reach another device: no remote copies, remote signals or barrier semaphores. Data moves between devices by JAX's collectives and lax.ppermute only.
A program may use at most 64 MiB of HBM per device.

v0:
```python
import jax
import jax.numpy as jnp
from jax import lax
from jax.sharding import PartitionSpec as P


def tanh_layer(value, tangents, laplacian, w_full, bias):
    feat_index = lax.axis_index("feat")
    half_width = value.shape[1]
    count_w, count_t = (tangents.shape[0], tangents.shape[1])
    stacked = jnp.stack([value, laplacian])
    w_rows = lax.dynamic_slice_in_dim(w_full, feat_index * half_width, half_width, 0)
    partial_vl = jnp.einsum("kbd,de->kbe", stacked, w_rows, preferred_element_type=jnp.float32)
    partial_grad = jnp.dot(
        tangents.reshape(count_w * count_t, half_width), w_rows, preferred_element_type=jnp.float32
    ).reshape(count_w, count_t, w_full.shape[1])
    summed, grad_pre = (
        lax.psum_scatter(partial_vl, "feat", scatter_dimension=2, tiled=True),
        lax.psum_scatter(partial_grad, "feat", scatter_dimension=2, tiled=True),
    )
    pre_act = summed[0] + bias
    lap_pre = summed[1]
    hidden = jnp.tanh(pre_act)
    slope = 1.0 - hidden * hidden
    bend = -2.0 * hidden * slope
    return (hidden, slope, bend, grad_pre, lap_pre)


def own_half(vector, half_width):
    return lax.dynamic_slice_in_dim(vector, lax.axis_index("feat") * half_width, half_width, 0)


def per_device(value_in, tang_in, lap_in, w_first, b_first, w_second, b_second, readout):
    full_first, full_second = (
        lax.all_gather(w_first, ("walker", "tangent", "feat"), axis=0, tiled=True),
        lax.all_gather(w_second, ("walker", "tangent", "feat"), axis=0, tiled=True),
    )
    half_width = value_in.shape[1]
    value_start, lap_start, tangents_in = (value_in, lap_in, tang_in)
    bias_one = own_half(b_first, half_width)
    bias_two = own_half(b_second, half_width)
    read_weights = own_half(readout, half_width)
    hidden, slope, bend, grad_pre, lap_pre = tanh_layer(
        value_start, tangents_in, lap_start, full_first, bias_one
    )
    curv_first = lax.psum(jnp.sum(grad_pre * grad_pre, axis=1), "tangent")
    value_two = hidden.astype(jnp.bfloat16)
    tang_two = (slope[:, None, :] * grad_pre).astype(jnp.bfloat16)
    lap_two = (slope * lap_pre + bend * curv_first).astype(jnp.bfloat16)
    hidden, slope, bend, grad_pre, lap_pre = tanh_layer(
        value_two, tang_two, lap_two, full_second, bias_two
    )
    amp_part = jnp.sum(read_weights * hidden, axis=-1)
    grad_part = jnp.sum(grad_pre * (read_weights * slope)[:, None, :], axis=-1)
    local_squares = jnp.sum(grad_pre * grad_pre, axis=1)
    curv_second = lax.psum(local_squares, "tangent")
    lap_part = jnp.sum(read_weights * (slope * lap_pre + bend * curv_second), axis=-1)
    log_amplitude, gradient, laplace = lax.psum((amp_part, grad_part, lap_part), "feat")
    squares = lax.psum(jnp.sum(gradient * gradient, axis=-1), "tangent")
    kinetic = -0.5 * (laplace + squares)
    return (log_amplitude, gradient, kinetic)


def solution(mesh):
    placed = (
        P("walker", "feat"),
        P("walker", "tangent", "feat"),
        P("walker", "feat"),
        P(("walker", "tangent", "feat"), None),
        P(),
        P(("walker", "tangent", "feat"), None),
        P(),
        P(),
    )
    return jax.shard_map(
        per_device,
        mesh=mesh,
        in_specs=placed,
        out_specs=(P("walker"), P("walker", "tangent"), P("walker")),
        check_vma=False,
    )
```

profile of v0, /device:TPU:1, one launch (start us, length us, event | category | flops | bytes accessed | tf_op | source)
XLA Modules:
  0.0 270.8 jit_solution(8628064673603538799)
XLA Ops:
  7.2 73.3 %all-gather = bf16[256,2,512]{2,1,0:T(2,128)(2,1)S(1)} all-gather(bf16[1,2,512]{2,1,0:T(2,128)(2,1)} %bitcast.67), channel_id=1, replica_groups=mesh['walker'=16,'tangent'=8,'feat'=2] {'walker','tangent','feat'}, dimensions={0}, use_global_device_ids=true | all-gather | bytes 526336 | tf_op jit(solution)/shard_map/all_gather | solution.py:35
  80.5 0.2 reshape.72
  80.7 1.6 fusion.5
  82.4 3.7 %convolution_bitcast_fusion = f32[3072,512]{0,1:T(8,128)} fusion(bf16[3072,256]{1,0:T(8,128)(2,1)S(1)} %bitcast.63, bf16[512,512]{1,0:T(8,128)(2,1)S(1)} %reshape.72, s32[]{:T(128)S(6)} %select_n.2), kind=kOutput, calls=%fused_computation | convolution fusion | flops 805306368 | bytes 8126468 | tf_op jit(solution)/shard_map/dot_general | solution.py:14
  86.1 6.6 %copy.13 = f32[3072,512]{1,0:T(8,128)} copy(f32[3072,512]{0,1:T(8,128)} %convolution_bitcast_fusion) | data formatting | bytes 12582912 | tf_op jit(solution)/shard_map/dot_general | solution.py:14
  92.8 0.6 copy-done.5
  93.5 65.6 %all-gather.1 = bf16[256,2,512]{2,1,0:T(2,128)(2,1)S(1)} all-gather(bf16[1,2,512]{2,1,0:T(2,128)(2,1)S(1)} %bitcast.68), channel_id=1, replica_groups=mesh['walker'=16,'tangent'=8,'feat'=2] {'walker','tangent','feat'}, dimensions={0}, use_global_device_ids=true | all-gather | bytes 526336 | tf_op jit(solution)/shard_map/all_gather | solution.py:36
  159.1 0.2 reshape.74
  159.3 0.8 tanh_convert_fusion
  160.2 2.2 multiply_reduce_fusion.2
  162.4 22.1 %psum.42 = f32[32,256]{1,0:T(8,128)S(1)} all-reduce(f32[32,256]{1,0:T(8,128)S(1)} %multiply_reduce_fusion.2), channel_id=1, replica_groups=mesh['walker'=16,'tangent'=8,'feat'=2] {'tangent'}, use_global_device_ids=true, to_apply=%region_3.0 | all-reduce | flops 8192 | bytes 65536 | tf_op jit(solution)/shard_map/psum | solution.py:46
  184.6 0.8 fusion.3
  185.5 5.5 %fusion = f32[32,96,512]{2,1,0:T(8,128)} fusion(f32[32,96,256]{2,1,0:T(8,128)} %reduce-scatter.7.cloned.1.call-done, f32[32,256]{1,0:T(8,128)S(1)} %get-tuple-element.11, bf16[512,512]{1,0:T(8,128)(2,1)S(1)} %reshape.74, s32[]{:T(128)S(6)} %select_n.2), kind=kOutput, calls=%fused_computation.5 | convolution fusion | flops 806879232 | bytes 9732100 | tf_op jit(solution)/shard_map/dot_general | solution.py:14
  191.1 0.7 copy-done.6
  191.9 9.7 %reduce-scatter.9.cloned.1.call-done = f32[2,32,256]{2,1,0:T(8,128)} async-done(((f32[2,32,512]{2,1,0:T(8,128)}), f32[2,32,256]{2,1,0:T(8,128)}) %reduce-scatter.9.cloned.1.call-update) | async-done | bytes 65552 | tf_op jit(solution)/shard_map/reduce_scatter | solution.py:18
  201.6 0.8 fusion.27
  202.4 21.9 %reduce-scatter.11.cloned.1.call-done = f32[32,96,256]{2,1,0:T(8,128)} async-done(((f32[32,96,512]{2,1,0:T(8,128)}), f32[32,96,256]{2,1,0:T(8,128)}) %reduce-scatter.11.cloned.1.call-update) | async-done | bytes 3145744 | tf_op jit(solution)/shard_map/reduce_scatter | solution.py:19
  224.4 2.5 multiply_reduce_fusion
  226.9 3.6 %psum.44 = f32[32,96]{1,0:T(8,128)S(1)} all-reduce(f32[32,96]{1,0:T(8,128)S(1)} %get-tuple-element.4), channel_id=1, replica_groups=mesh['walker'=16,'tangent'=8,'feat'=2] {'feat'}, use_global_device_ids=true, to_apply=%region_9.0 | all-reduce | flops 3072 | bytes 24576 | tf_op jit(solution)/shard_map/psum | solution.py:58
  230.5 0.1 multiply_reduce_fusion.4
  230.6 23.2 %all-reduce = (f32[32,256]{1,0:T(8,128)S(1)}, f32[32]{0:T(128)S(1)}) all-reduce(f32[32,256]{1,0:T(8,128)S(1)} %get-tuple-element.3, f32[32]{0:T(128)S(1)} %multiply_reduce_fusion.4), channel_id=1, replica_groups=mesh['walker'=16,'tangent'=8,'feat'=2] {'tangent'}, use_global_device_ids=true, to_apply=%region_11.0 | all-reduce | flops 8224 | bytes 65792 | tf_op jit(solution)/shard_map/psum | solution.py:56
  253.8 0.1 fusion.14
  253.9 9.9 %all-reduce.1 = (f32[32]{0:T(128)}, f32[32]{0:T(128)S(1)}) all-reduce(f32[32]{0:T(128)S(1)} %get-tuple-element.6, f32[32]{0:T(128)S(1)} %get-tuple-element.5), channel_id=1, replica_groups=mesh['walker'=16,'tangent'=8,'feat'=2] {'feat'}, use_global_device_ids=true, to_apply=%region_6.0 | all-reduce | flops 64 | bytes 512 | tf_op jit(solution)/shard_map/psum | solution.py:58
  263.8 0.5 add_multiply_fusion
  (28 shorter events, 0.5 us)
Async XLA Ops:
  7.2 75.2 %copy-start = (bf16[32,96,256]{2,1,0:T(8,128)(2,1)S(1)}, bf16[32,96,256]{2,1,0:T(8,128)(2,1)}, u32[]{:S(2)}) copy-start(bf16[32,96,256]{2,1,0:T(8,128)(2,1)} %param.9) | copy-start | bytes 4718596
  7.2 152.1 %reduce-scatter.5.cloned.1.call-start = ((), (), s32[]{:S(2)}) async-start(), calls=%async_computation.4 | async-start | bytes 196608 | tf_op jit(solution)/shard_map/reduce_scatter | solution.py:18
  82.3 77.9 %reduce-scatter.7.cloned.1.call-start = ((), (), s32[]{:S(2)}) async-start(), calls=%async_computation.5 | async-start | bytes 9437184 | tf_op jit(solution)/shard_map/reduce_scatter | solution.py:19
  92.7 0.7 copy-start.5
  92.7 0.8 copy-start.4
  92.7 108.9 %reduce-scatter.9.cloned.1.call-start = ((), (), s32[]{:S(2)}) async-start(), calls=%async_computation.6 | async-start | bytes 196608 | tf_op jit(solution)/shard_map/reduce_scatter | solution.py:18
  159.3 25.2 %copy-start.1 = (f32[2,32,256]{2,1,0:T(8,128)S(1)}, f32[2,32,256]{2,1,0:T(8,128)}, u32[]{:S(2)}) copy-start(f32[2,32,256]{2,1,0:T(8,128)} %reduce-scatter.5.cloned.1.call-done) | copy-start | bytes 196612
  185.4 38.9 %reduce-scatter.11.cloned.1.call-start = ((), (), s32[]{:S(2)}) async-start(), calls=%async_computation.7 | async-start | bytes 9437184 | tf_op jit(solution)/shard_map/reduce_scatter | solution.py:19
  191.0 0.7 copy-start.6
  191.0 0.8 copy-start.7
  201.6 52.2 %copy-start.2 = (f32[2,32,256]{2,1,0:T(8,128)S(1)}, f32[2,32,256]{2,1,0:T(8,128)}, u32[]{:S(2)}) copy-start(f32[2,32,256]{2,1,0:T(8,128)} %reduce-scatter.9.cloned.1.call-done) | copy-start | bytes 196612
  230.5 33.8 %copy-start.3 = (f32[32,96]{1,0:T(8,128)}, f32[32,96]{1,0:T(8,128)S(1)}, u32[]{:S(2)}) copy-start(f32[32,96]{1,0:T(8,128)S(1)} %psum.44) | copy-start | bytes 36868
Sparse Core Ops, SparseCore 0:
  82.5 9.7 reduce-scatter.4
  94.8 20.2 reduce-scatter.6
  185.6 15.9 reduce-scatter.8
  204.0 20.3 reduce-scatter.10
where the time goes:
time: 271 us
  blocking collectives  198 us (73%)
  waiting for transfers between devices  31.8 us (12%)
  between operations  13.9 us (5%)
  matrix products  11.6 us (4%)
  local copies, waits for them, and re-layouts  8.51 us (3%)
  other arithmetic  7.18 us (3%)
    all_gather x1, blocking collectives, per_device(): lax.all_gather(w_first, ('walker', 'tangent', 'feat'), axis=0, tiled=True)  73.3 us
    all_gather x1, blocking collectives, per_device(): lax.all_gather(w_second, ('walker', 'tangent', 'feat'), axis=0, tiled=True)  65.6 us
    psum x1, blocking collectives, per_device(): curv_second = lax.psum(local_squares, 'tangent')  23.2 us
    psum x1, blocking collectives, per_device(): curv_first = lax.psum(jnp.sum(grad_pre * grad_pre, axis=1), 'tangent')  22.1 us
    reduce_scatter x2, waiting for transfers between devices, tanh_layer(): lax.psum_scatter(partial_grad, 'feat', scatter_dimension=2, tiled=True)  21.9 us
    psum x2, blocking collectives, per_device(): lax.psum((amp_part, grad_part, lap_part), 'feat')  13.5 us
    reduce_scatter x2, waiting for transfers between devices, tanh_layer(): lax.psum_scatter(partial_vl, 'feat', scatter_dimension=2, tiled=True)  9.74 us
    dot_general x2, matrix products, tanh_layer(): jnp.dot(tangents.reshape(count_w * count_t, half_width), w_rows, preferre...  9.24 us
  transfers between devices with their start and end apart: 4, of which 2 were waited for; matrix products, arithmetic and copies ran while one was open for 7% of the time, Pallas kernels for 0%

commit v1 on v0

--- a/solution.py
+++ b/solution.py
@@ -1,7 +1,23 @@
+import functools
 import jax
 import jax.numpy as jnp
 from jax import lax
 from jax.sharding import PartitionSpec as P
+
+
+def show_rows_now(xs, which_axis, dim_no):
+    pieces_in = []
+    for _ in range(lax.axis_size(which_axis)):
+        pieces_in.append(xs)
+    return jnp.concatenate(
+        lax.all_to_all(jnp.stack(pieces_in), axis_name=which_axis, split_axis=0, concat_axis=0),
+        axis=dim_no,
+    )
+
+
+solve_halves_by_axis = functools.partial(
+    show_rows_now, which_axis=("walker", "tangent", "feat"), dim_no=0
+)
 
 
 def tanh_layer(value, tangents, laplacian, w_full, bias):
@@ -33,7 +49,7 @@
 def per_device(value_in, tang_in, lap_in, w_first, b_first, w_second, b_second, readout):
     full_first, full_second = (
         lax.all_gather(w_first, ("walker", "tangent", "feat"), axis=0, tiled=True),
-        lax.all_gather(w_second, ("walker", "tangent", "feat"), axis=0, tiled=True),
+        solve_halves_by_axis(w_second),
     )
     half_width = value_in.shape[1]
     value_start, lap_start, tangents_in = (value_in, lap_in, tang_in)

time: 271 us -> 233 us (0.86)
  blocking collectives: 198 us -> 131 us
  waiting for transfers between devices: 31.8 us -> 51.3 us
  starting transfers between devices: 0.16 us -> 8.1 us
    all_gather x1 -> x0, blocking collectives: 65.6 us -> none  [per_device(): lax.all_gather(w_second, ('walker', 'tangent', 'feat'), axis=0, tiled=True)]
    all_to_all x0 -> x1, waiting for transfers between devices: none -> 20.4 us  [show_rows_now(): lax.all_to_all(jnp.stack(pieces_in), axis_name=which_axis, split_axis=0,...]
    all_to_all x0 -> x1, starting transfers between devices: none -> 7.94 us  [show_rows_now(): lax.all_to_all(jnp.stack(pieces_in), axis_name=which_axis, split_axis=0,...]
  transfers between devices with their start and end apart: 4 -> 5, of which waited for: 2 -> 3; matrix products, arithmetic and copies ran while one was open for 7% -> 8% of each run, Pallas kernels for 0% -> 0%
where the time goes in v1:
time: 233 us; the launch traced here: 232 us
  blocking collectives  131 us (56%)
  waiting for transfers between devices  51.3 us (22%)
  between operations  13.9 us (6%)
  matrix products  11.6 us (5%)
  local copies, waits for them, and re-layouts  9.63 us (4%)
  starting transfers between devices  8.1 us (3%)
  other arithmetic  7.19 us (3%)
    all_gather x1, blocking collectives, per_device(): lax.all_gather(w_first, ('walker', 'tangent', 'feat'), axis=0, tiled=True)  73.3 us
    psum x1, blocking collectives, per_device(): curv_second = lax.psum(local_squares, 'tangent')  23.1 us
    reduce_scatter x2, waiting for transfers between devices, tanh_layer(): lax.psum_scatter(partial_grad, 'feat', scatter_dimension=2, tiled=True)  21.9 us
    psum x1, blocking collectives, per_device(): curv_first = lax.psum(jnp.sum(grad_pre * grad_pre, axis=1), 'tangent')  20.6 us
    all_to_all x1, waiting for transfers between devices, show_rows_now(): lax.all_to_all(jnp.stack(pieces_in), axis_name=which_axis, split_axis=0,...  20.4 us
    psum x2, blocking collectives, per_device(): lax.psum((amp_part, grad_part, lap_part), 'feat')  13.5 us
    dot_general x2, matrix products, tanh_layer(): jnp.dot(tangents.reshape(count_w * count_t, half_width), w_rows, preferre...  9.24 us
    reduce_scatter x2, waiting for transfers between devices, tanh_layer(): lax.psum_scatter(partial_vl, 'feat', scatter_dimension=2, tiled=True)  8.91 us
  transfers between devices with their start and end apart: 5, of which 3 were waited for; matrix products, arithmetic and copies ran while one was open for 8% of the time, Pallas kernels for 0%

profile of v1, /device:TPU:1, one launch (start us, length us, event | category | flops | bytes accessed | tf_op | source)
XLA Modules:
  0.0 232.3 jit_solution(4439013841642403656)
XLA Ops:
  7.2 73.3 %all-gather = bf16[256,2,512]{2,1,0:T(2,128)(2,1)S(1)} all-gather(bf16[1,2,512]{2,1,0:T(2,128)(2,1)} %bitcast.66), channel_id=1, replica_groups=mesh['walker'=16,'tangent'=8,'feat'=2] {'walker','tangent','feat'}, dimensions={0}, use_global_device_ids=true | all-gather | bytes 526336 | tf_op jit(solution)/shard_map/all_gather | solution.py:51
  80.5 0.2 reshape.78
  80.7 1.6 fusion.5
  82.4 3.7 %convolution_bitcast_fusion = f32[3072,512]{0,1:T(8,128)} fusion(bf16[3072,256]{1,0:T(8,128)(2,1)S(1)} %bitcast.62, bf16[512,512]{1,0:T(8,128)(2,1)S(1)} %reshape.78, s32[]{:T(128)S(6)} %select_n.2), kind=kOutput, calls=%fused_computation | convolution fusion | flops 805306368 | bytes 8126468 | tf_op jit(solution)/shard_map/dot_general | solution.py:30
  86.1 6.6 %copy.13 = f32[3072,512]{1,0:T(8,128)} copy(f32[3072,512]{0,1:T(8,128)} %convolution_bitcast_fusion) | data formatting | bytes 12582912 | tf_op jit(solution)/shard_map/dot_general | solution.py:30
  92.7 0.7 copy-done.4
  93.4 1.1 stack.17
  94.4 7.9 %all-to-all-start = ((bf16[256,2,512]{2,1,0:T(2,128)(2,1)}), bf16[256,2,512]{2,1,0:T(2,128)(2,1)S(1)}, u32[]{:S(2)}, u32[]{:S(2)}) async-start(bf16[256,2,512]{2,1,0:T(2,128)(2,1)} %stack.17), calls=%async_computation.2 | async-start | bytes 1048576 | tf_op jit(solution)/shard_map/all_to_all | solution.py:13
  102.5 0.8 tanh_convert_fusion
  103.4 20.4 %all-to-all-done = bf16[256,2,512]{2,1,0:T(2,128)(2,1)S(1)} async-done(((bf16[256,2,512]{2,1,0:T(2,128)(2,1)}), bf16[256,2,512]{2,1,0:T(2,128)(2,1)S(1)}, u32[]{:S(2)}, u32[]{:S(2)}) %all-to-all-start) | async-done | bytes 524320 | tf_op jit(solution)/shard_map/all_to_all | solution.py:13
  123.8 0.2 reshape.76
  124.0 2.2 multiply_reduce_fusion.2
  126.2 20.6 %psum.42 = f32[32,256]{1,0:T(8,128)S(1)} all-reduce(f32[32,256]{1,0:T(8,128)S(1)} %multiply_reduce_fusion.2), channel_id=1, replica_groups=mesh['walker'=16,'tangent'=8,'feat'=2] {'tangent'}, use_global_device_ids=true, to_apply=%region_3.0 | all-reduce | flops 8192 | bytes 65536 | tf_op jit(solution)/shard_map/psum | solution.py:62
  146.9 0.8 fusion.3
  147.8 5.5 %fusion = f32[32,96,512]{2,1,0:T(8,128)} fusion(f32[32,96,256]{2,1,0:T(8,128)} %reduce-scatter.7.cloned.1.call-done, f32[32,256]{1,0:T(8,128)S(1)} %get-tuple-element.11, bf16[512,512]{1,0:T(8,128)(2,1)S(1)} %reshape.76, s32[]{:T(128)S(6)} %select_n.2), kind=kOutput, calls=%fused_computation.5 | convolution fusion | flops 806879232 | bytes 9732100 | tf_op jit(solution)/shard_map/dot_general | solution.py:30
  153.3 0.7 copy-done.6
  154.2 8.9 %reduce-scatter.9.cloned.1.call-done = f32[2,32,256]{2,1,0:T(8,128)} async-done(((f32[2,32,512]{2,1,0:T(8,128)}), f32[2,32,256]{2,1,0:T(8,128)}) %reduce-scatter.9.cloned.1.call-update) | async-done | bytes 65552 | tf_op jit(solution)/shard_map/reduce_scatter | solution.py:34
  163.1 0.8 fusion.27
  163.9 21.9 %reduce-scatter.11.cloned.1.call-done = f32[32,96,256]{2,1,0:T(8,128)} async-done(((f32[32,96,512]{2,1,0:T(8,128)}), f32[32,96,256]{2,1,0:T(8,128)}) %reduce-scatter.11.cloned.1.call-update) | async-done | bytes 3145744 | tf_op jit(solution)/shard_map/reduce_scatter | solution.py:35
  185.8 2.5 %multiply_reduce_fusion = (f32[32,256]{1,0:T(8,128)S(1)}, f32[32,96]{1,0:T(8,128)S(1)}) fusion(f32[32,96,256]{2,1,0:T(8,128)} %reduce-scatter.11.cloned.1.call-done, f32[32,256]{1,0:T(8,128)S(1)} %fusion.27), kind=kLoop, calls=%fused_computation.1 | loop fusion | flops 3134464 | bytes 3223552 | tf_op jit(solution)/shard_map/reduce_sum | solution.py:71
  188.3 3.6 %psum.44 = f32[32,96]{1,0:T(8,128)S(1)} all-reduce(f32[32,96]{1,0:T(8,128)S(1)} %get-tuple-element.4), channel_id=1, replica_groups=mesh['walker'=16,'tangent'=8,'feat'=2] {'feat'}, use_global_device_ids=true, to_apply=%region_9.0 | all-reduce | flops 3072 | bytes 24576 | tf_op jit(solution)/shard_map/psum | solution.py:74
  192.0 23.1 %all-reduce = (f32[32,256]{1,0:T(8,128)S(1)}, f32[32]{0:T(128)S(1)}) all-reduce(f32[32,256]{1,0:T(8,128)S(1)} %get-tuple-element.3, f32[32]{0:T(128)S(1)} %multiply_reduce_fusion.4), channel_id=1, replica_groups=mesh['walker'=16,'tangent'=8,'feat'=2] {'tangent'}, use_global_device_ids=true, to_apply=%region_11.0 | all-reduce | flops 8224 | bytes 65792 | tf_op jit(solution)/shard_map/psum | solution.py:72
  215.3 9.9 %all-reduce.1 = (f32[32]{0:T(128)}, f32[32]{0:T(128)S(1)}) all-reduce(f32[32]{0:T(128)S(1)} %get-tuple-element.6, f32[32]{0:T(128)S(1)} %get-tuple-element.5), channel_id=1, replica_groups=mesh['walker'=16,'tangent'=8,'feat'=2] {'feat'}, use_global_device_ids=true, to_apply=%region_6.0 | all-reduce | flops 64 | bytes 512 | tf_op jit(solution)/shard_map/psum | solution.py:74
  225.2 0.5 add_multiply_fusion
  (30 shorter events, 0.8 us)
Async XLA Ops:
  7.2 75.2 %copy-start = (bf16[32,96,256]{2,1,0:T(8,128)(2,1)S(1)}, bf16[32,96,256]{2,1,0:T(8,128)(2,1)}, u32[]{:S(2)}) copy-start(bf16[32,96,256]{2,1,0:T(8,128)(2,1)} %param.9) | copy-start | bytes 4718596
  7.2 95.4 %reduce-scatter.5.cloned.1.call-start = ((), (), s32[]{:S(2)}) async-start(), calls=%async_computation.5 | async-start | bytes 196608 | tf_op jit(solution)/shard_map/reduce_scatter | solution.py:34
  82.3 41.7 %reduce-scatter.7.cloned.1.call-start = ((), (), s32[]{:S(2)}) async-start(), calls=%async_computation.6 | async-start | bytes 9437184 | tf_op jit(solution)/shard_map/reduce_scatter | solution.py:35
  92.7 0.7 copy-start.4
  92.7 9.7 %copy-start.5 = (f32[512]{0:T(512)S(1)}, f32[512]{0:T(512)}, u32[]{:S(2)}) copy-start(f32[512]{0:T(512)} %param.12) | copy-start | bytes 6148
  94.4 29.3 %all-to-all-start = ((bf16[256,2,512]{2,1,0:T(2,128)(2,1)}), bf16[256,2,512]{2,1,0:T(2,128)(2,1)S(1)}, u32[]{:S(2)}, u32[]{:S(2)}) async-start(bf16[256,2,512]{2,1,0:T(2,128)(2,1)} %stack.17), calls=%async_computation.2 | async-start | bytes 1048576 | tf_op jit(solution)/shard_map/all_to_all | solution.py:13
  102.4 60.7 %reduce-scatter.9.cloned.1.call-start = ((), (), s32[]{:S(2)}) async-start(), calls=%async_computation.7 | async-start | bytes 196608 | tf_op jit(solution)/shard_map/reduce_scatter | solution.py:34
  102.5 44.3 %copy-start.1 = (f32[2,32,256]{2,1,0:T(8,128)S(1)}, f32[2,32,256]{2,1,0:T(8,128)}, u32[]{:S(2)}) copy-start(f32[2,32,256]{2,1,0:T(8,128)} %reduce-scatter.5.cloned.1.call-done) | copy-start | bytes 196612
  147.7 38.1 %reduce-scatter.11.cloned.1.call-start = ((), (), s32[]{:S(2)}) async-start(), calls=%async_computation.8 | async-start | bytes 9437184 | tf_op jit(solution)/shard_map/reduce_scatter | solution.py:35
  153.3 0.7 copy-start.6
  153.3 0.8 copy-start.7
  163.1 52.1 %copy-start.2 = (f32[2,32,256]{2,1,0:T(8,128)S(1)}, f32[2,32,256]{2,1,0:T(8,128)}, u32[]{:S(2)}) copy-start(f32[2,32,256]{2,1,0:T(8,128)} %reduce-scatter.9.cloned.1.call-done) | copy-start | bytes 196612
  191.9 33.8 %copy-start.3 = (f32[32,96]{1,0:T(8,128)}, f32[32,96]{1,0:T(8,128)S(1)}, u32[]{:S(2)}) copy-start(f32[32,96]{1,0:T(8,128)S(1)} %psum.44) | copy-start | bytes 36868
Sparse Core Ops, SparseCore 0:
  82.5 9.7 reduce-scatter.4
  94.8 20.2 reduce-scatter.6
  147.8 15.1 reduce-scatter.8
  165.5 20.2 reduce-scatter.10
